TPU v7x, 32 devices: a whole 2x2x4 slice. The times are simulated.
32 devices in a mesh: req: 32 (over z, y, x, core).
Axes of the slice: x: 2, y: 2, z: 4, core: 2. Of those that a mesh axis runs over, the one named last changes fastest.
Arguments:
- hidden_in: bfloat16 [16384, 2048], P('req'), may hold values from -6 to 6
- qkv: bfloat16 [16384, 6144], P('req'), may hold values from -400 to 400
- cache: bfloat16 [128, 128, 4096], P('req'), may hold values from -400 to 400
- lengths: int32 [128], P('req'), may hold values from 2 to 128, as said below
- prefill_flag: int32 [32], P('req'), may hold values 0 or 1
- cache_slot: int32 [128], P('req'), may hold values from 0 to 127, as said below
- slot_owner: int32 [128], P('req'), may hold values from 0 to 127, as said below
- out_weight: bfloat16 [2048, 2048], replicated, may hold values from -0.125 to 0.125
Outputs:
- layer_out: bfloat16 [16384, 2048], P('req')
Inputs may be any that keep to these rules, and one draw needn't show every extreme that they name: Each slot stores exactly one request's cache; of each device's 4 requests, at least half have their cache in a slot of their own device, drawn which; slot_owner[cache_slot[r]] = r. `slot_owner`: the inverse of cache_slot. `lengths`: some slot holds exactly 128 valid positions.
All inputs are finite; a program needn't handle non-finite values. No bound on the sum of `prefill_flag` on one device may be relied on, other than what follows from the above.
Results may differ from a plain program's by a relative error of at most 0.0034.
Values may be sent and summed in bfloat16 or wider, within the bound.
A program may use at most 128 MiB of HBM per device.

v0:
```python
import math

import jax
import jax.numpy as jnp
from jax import lax
from jax.sharding import PartitionSpec as P

D = 2048
H = 16
HD = 128
TOK_DEV = 512
RD = 4
LMAX = 128


def prefill_attention(block):
    score_scale = 1.0 / math.sqrt(HD)
    queries = block[:, :D].reshape(TOK_DEV, H, HD)
    keys_new = block[:, D : 2 * D].reshape(TOK_DEV, H, HD)
    values_new = block[:, 2 * D :].reshape(TOK_DEV, H, HD)
    scores = (
        jnp.einsum("qhd,khd->hqk", queries, keys_new, preferred_element_type=jnp.float32)
        * score_scale
    )
    causal = jnp.arange(TOK_DEV)[:, None] >= jnp.arange(TOK_DEV)[None, :]
    scores = jnp.where(causal[None], scores, -jnp.inf)
    top_score = jnp.max(scores, axis=-1, keepdims=True)
    expon = jnp.exp(scores - top_score)
    totals = jnp.sum(expon, axis=-1)
    summed = jnp.einsum(
        "hqk,khd->qhd", expon.astype(jnp.bfloat16), values_new, preferred_element_type=jnp.float32
    )
    result = summed / jnp.transpose(totals)[:, :, None]
    return result.reshape(TOK_DEV, D).astype(jnp.bfloat16)


def holder_partial(queries, cache, lengths):
    score_scale = 1.0 / math.sqrt(HD)
    query_heads = queries.reshape(RD, H, HD)
    cache_keys = cache[:, :, :D].reshape(RD, LMAX, H, HD)
    cache_values = cache[:, :, D:].reshape(RD, LMAX, H, HD)
    scores = (
        jnp.einsum("rhd,rlhd->rhl", query_heads, cache_keys, preferred_element_type=jnp.float32)
        * score_scale
    )
    valid = jnp.arange(LMAX, dtype=jnp.int32)[None, None, :] < lengths[:, None, None]
    scores = jnp.where(valid, scores, -jnp.inf)
    cache_max = jnp.max(scores, axis=-1)
    expon = jnp.exp(scores - cache_max[..., None])
    cache_total = jnp.sum(expon, axis=-1)
    cache_out = jnp.einsum(
        "rhl,rlhd->rhd",
        expon.astype(jnp.bfloat16),
        cache_values,
        preferred_element_type=jnp.float32,
    )
    return (cache_out.reshape(RD, D), cache_max, cache_total)


def combine_own(request_rows, cache_out, cache_max, cache_total):
    score_scale = 1.0 / math.sqrt(HD)
    query_heads = request_rows[:, :D].reshape(RD, H, HD).astype(jnp.float32)
    keys_new = request_rows[:, D : 2 * D].reshape(RD, H, HD).astype(jnp.float32)
    values_new = request_rows[:, 2 * D :].reshape(RD, H, HD).astype(jnp.float32)
    own_score = jnp.sum(query_heads * keys_new, axis=-1) * score_scale
    joint_max = jnp.maximum(cache_max, own_score)
    cache_factor = jnp.exp(cache_max - joint_max)
    own_factor = jnp.exp(own_score - joint_max)
    numer = (
        cache_out.reshape(RD, H, HD) * cache_factor[..., None] + own_factor[..., None] * values_new
    )
    denom = cache_total * cache_factor + own_factor
    return (numer / denom[..., None]).reshape(RD, D).astype(jnp.bfloat16)


def local(hidden_in, qkv, cache, lengths, prefill_flag, cache_slot, slot_owner, out_weight):
    request_rows = qkv[:RD]
    every_query = lax.all_gather(request_rows[:, :D], "req", axis=0, tiled=True)
    held_queries = every_query[slot_owner]
    part_out, part_max, part_total = holder_partial(held_queries, cache, lengths)
    every_out, every_max, every_total = (
        lax.all_gather(part_out.astype(jnp.bfloat16), "req", axis=0, tiled=True).astype(
            part_out.dtype
        ),
        lax.all_gather(part_max.astype(jnp.bfloat16), "req", axis=0, tiled=True).astype(
            part_max.dtype
        ),
        lax.all_gather(part_total.astype(jnp.bfloat16), "req", axis=0, tiled=True).astype(
            part_total.dtype
        ),
    )
    decode_att = combine_own(
        request_rows, every_out[cache_slot], every_max[cache_slot], every_total[cache_slot]
    )
    is_prefill = prefill_flag[0] == 1

    def prefill_path(block):
        attended = prefill_attention(block)
        return jnp.dot(attended, out_weight, preferred_element_type=jnp.float32).astype(
            jnp.bfloat16
        )

    def decode_path(block):
        live = jnp.dot(decode_att, out_weight, preferred_element_type=jnp.float32).astype(
            jnp.bfloat16
        )
        return jnp.concatenate([live, jnp.zeros((TOK_DEV - RD, D), jnp.bfloat16)], axis=0)

    projected = lax.cond(is_prefill, prefill_path, decode_path, qkv)
    summed = hidden_in.astype(jnp.float32) + projected.astype(jnp.float32)
    return summed.astype(jnp.bfloat16)


def solution(mesh):
    placed = (
        P("req", None),
        P("req", None),
        P("req", None, None),
        P("req"),
        P("req"),
        P("req"),
        P("req"),
        P(),
    )
    return jax.shard_map(
        local, mesh=mesh, in_specs=placed, out_specs=P("req", None), check_vma=False
    )
```

profile of v0, /device:TPU:0, one launch (start us, length us, event | category | flops | bytes accessed | tf_op | source)
XLA Modules:
  0.0 231.2 jit_solution(15579366147625669525)
XLA Ops:
  0.7 0.7 iota_compare_fusion.1
  1.4 0.7 compare_select_fusion
  2.0 0.7 compare_select_fusion.1
  2.7 0.8 slice_bitcast_fusion.1
  3.5 0.8 multiply_bitcast_fusion
  4.3 0.1 bitcast_reduce_fusion
  4.4 44.6 %all-gather = bf16[32,4,2048]{2,1,0:T(4,128)(2,1)S(1)} all-gather(bf16[1,4,2048]{2,1,0:T(4,128)(2,1)S(1)} %slice_bitcast_fusion.1), channel_id=1, replica_groups=mesh['req'=32] {'req'}, dimensions={0}, use_global_device_ids=true | all-gather | bytes 540672 | tf_op jit(solution)/shard_map/all_gather | solution.py:78
  49.0 0.1 reshape.136
  49.1 0.6 gather_fusion
  49.7 4.9 %slice_bitcast_fusion = (bf16[4,16,16,8,128]{4,3,2,1,0:T(8,128)(2,1)}, bf16[4,128,2048]{2,1,0:T(8,128)(2,1)}) fusion(bf16[4,128,4096]{2,1,0:T(8,128)(2,1)} %param.12), kind=kLoop, calls=%fused_computation.27 | loop fusion | bytes 8388608
  54.6 3.0 %copy.32 = bf16[4,128,2048]{1,2,0:T(8,128)(2,1)S(1)} copy(bf16[4,128,2048]{2,1,0:T(8,128)(2,1)} %get-tuple-element.38) | data formatting | bytes 4194304 | tf_op jit(solution)/shard_map/reshape | solution.py:40
  57.6 0.6 fusion.30
  58.2 0.1 fusion.21
  58.3 0.2 fusion.24
  58.5 2.2 fusion.15
  60.8 36.7 %all-gather.3 = bf16[32,4,16]{2,1,0:T(4,128)(2,1)S(1)} all-gather(bf16[1,4,16]{2,1,0:T(4,128)(2,1)S(1)} %bitcast.80), channel_id=1, replica_groups=mesh['req'=32] {'req'}, dimensions={0}, use_global_device_ids=true | all-gather | bytes 4224 | tf_op jit(solution)/shard_map/all_gather | solution.py:88
  97.5 38.0 %all-gather.2 = bf16[32,4,16]{2,1,0:T(4,128)(2,1)S(1)} all-gather(bf16[1,4,16]{2,1,0:T(4,128)(2,1)S(1)} %convert_bitcast_fusion.1), channel_id=1, replica_groups=mesh['req'=32] {'req'}, dimensions={0}, use_global_device_ids=true | all-gather | bytes 4224 | tf_op jit(solution)/shard_map/all_gather | solution.py:85
  135.5 0.6 gather_fusion.2
  136.0 0.6 gather_fusion.3
  136.7 0.1 broadcast_bitcast_fusion
  136.8 38.1 %all-gather.1 = bf16[32,4,2048]{2,1,0:T(4,128)(2,1)S(1)} all-gather(bf16[1,4,2048]{2,1,0:T(4,128)(2,1)S(1)} %reshape.137), channel_id=1, replica_groups=mesh['req'=32] {'req'}, dimensions={0}, use_global_device_ids=true | all-gather | bytes 540672 | tf_op jit(solution)/shard_map/all_gather | solution.py:82
  174.9 0.6 gather_fusion.1
  175.5 0.8 fusion.20
  176.3 50.8 %conditional.1 = (f32[512,2048]{1,0:T(8,128)}) conditional(s32[]{:T(128)} %bitcast.6, (bf16[4,2048]{1,0:T(4,128)(2,1)S(1)}, bf16[2048,2048]{1,0:T(8,128)(2,1)}) %tuple.13, (bf16[512,6144]{1,0:T(8,128)(2,1)}, bf16[2048,2048]{1,0:T(8,128)(2,1)}) %tuple.14), branch_computations={%region_3.4_spmd, %region_4.7_spmd} | conditional | flops 6493028352 | bytes 99778568 | solution.py:109
  176.5 0.1 iota_compare_fusion
  176.6 8.8 %copy.22 = bf16[512,6144]{0,1:T(8,128)(2,1)} copy(bf16[512,6144]{1,0:T(8,128)(2,1)} %get-tuple-element.27) | data formatting | bytes 12582912 | tf_op jit(solution)/shard_map
  185.4 4.6 %fusion.29 = (bf16[512,2048]{0,1:T(8,128)(2,1)S(1)}, bf16[512,2048]{0,1:T(8,128)(2,1)S(1)}, bf16[512,2048]{0,1:T(8,128)(2,1)}) fusion(bf16[512,6144]{0,1:T(8,128)(2,1)} %copy.22), kind=kLoop, calls=%fused_computation.58 | loop fusion | bytes 12582912 | tf_op jit(solution)/shard_map/cond/branch_1_fun/slice | solution.py:19
  190.0 7.5 %fusion = (f32[16,512]{1,0:T(8,128)S(1)}, f32[16,512,512]{1,2,0:T(8,128)}) fusion(pred[512,512]{0,1:T(8,128)(4,1)S(1)} %iota_compare_fusion, bf16[512,16,128]{0,2,1:T(8,128)(2,1)S(1)} %bitcast.72, bf16[512,16,128]{0,2,1:T(8,128)(2,1)S(1)} %bitcast.71), kind=kOutput, calls=%fused_computation.8 | convolution fusion | flops 1086316544 | bytes 21266432 | tf_op jit(solution)/shard_map/cond/branch_1_fun/qhd,khd->hqk/dot_general | solution.py:22
  197.5 9.1 %fusion.1 = f32[16,512]{1,0:T(8,128)S(1)} fusion(f32[16,512,512]{1,2,0:T(8,128)} %get-tuple-element.36, f32[16,512]{1,0:T(8,128)S(1)} %get-tuple-element.35, pred[512,512]{0,1:T(8,128)(4,1)S(1)} %iota_compare_fusion), kind=kLoop, calls=%fused_computation.9 | loop fusion | flops 16769024 | bytes 17104896 | tf_op jit(solution)/shard_map/cond/branch_1_fun/reduce_sum | solution.py:29
  206.7 10.9 %fusion.9 = bf16[512,16,128]{0,2,1:T(8,128)(2,1)S(1)} fusion(bf16[512,16,128]{0,2,1:T(8,128)(2,1)} %bitcast.73, f32[16,512,512]{1,2,0:T(8,128)} %get-tuple-element.36, f32[16,512]{1,0:T(8,128)S(1)} %get-tuple-element.35, pred[512,512]{0,1:T(8,128)(4,1)S(1)} %iota_compare_fusion, f32[512,16]{0,1:T(8,128)S(1)} %bitcast.78), kind=kOutput, calls=%fused_computation.17 | convolution fusion | flops 1092616192 | bytes 21299200 | tf_op jit(solution)/shard_map/cond/branch_1_fun/hqk,khd->qhd/dot_general | solution.py:30
  217.6 9.4 %fusion.10 = f32[512,2048]{1,0:T(8,128)} fusion(bf16[512,2048]{0,1:T(8,128)(2,1)S(1)} %bitcast.81, bf16[2048,2048]{1,0:T(8,128)(2,1)} %get-tuple-element.20), kind=kOutput, calls=%fused_computation.19 | convolution fusion | flops 4297064448 | bytes 14680064 | tf_op jit(solution)/shard_map/cond/branch_1_fun/dot_general | solution.py:99
  227.1 4.2 %add_convert_fusion = bf16[512,2048]{1,0:T(8,128)(2,1)} fusion(f32[512,2048]{1,0:T(8,128)} %get-tuple-element.43, bf16[512,2048]{1,0:T(8,128)(2,1)S(1)} %copy-done), kind=kLoop, calls=%fused_computation.23 | loop fusion | flops 3145728 | bytes 8388608 | tf_op jit(solution)/shard_map/convert_element_type | solution.py:111
  (13 shorter events, 0.2 us)
Async XLA Ops:
  176.3 50.8 %copy-start = (bf16[512,2048]{1,0:T(8,128)(2,1)S(1)}, bf16[512,2048]{1,0:T(8,128)(2,1)}, u32[]{:S(2)}) copy-start(bf16[512,2048]{1,0:T(8,128)(2,1)} %param.10) | copy-start | bytes 6291460
where the time goes:
time: 232 us; the launch traced here: 231 us
  blocking collectives  157 us (68%)
  matrix products  30.8 us (13%)
  local copies, waits for them, and re-layouts  24.7 us (11%)
  other arithmetic  17.4 us (7%)
    all_gather x1, blocking collectives, local(): every_query = lax.all_gather(request_rows[:, :D], 'req', axis=0, tiled=True)  44.6 us
    all_gather x1, blocking collectives, local(): lax.all_gather(part_out.astype(jnp.bfloat16), 'req', axis=0, tiled=True)  38.1 us
    all_gather x1, blocking collectives, local(): lax.all_gather(part_max.astype(jnp.bfloat16), 'req', axis=0, tiled=True)  38 us
    all_gather x1, blocking collectives, local(): lax.all_gather(part_total.astype(jnp.bfloat16), 'req', axis=0, tiled=True)  36.7 us
    dot_general x1, matrix products, prefill_attention(): jnp.einsum('hqk,khd->qhd', expon.astype(jnp.bfloat16), values_new, prefer...  10.9 us
    dot_general x1, matrix products, prefill_path(): jnp.dot(attended, out_weight, preferred_element_type=jnp.float32)  9.44 us
    reduce_sum x1, other arithmetic, prefill_attention(): totals = jnp.sum(expon, axis=-1)  9.15 us
    another operation x1, local copies, waits for them, and re-layouts  8.85 us

commit v1 on v0

v1 whole, which is shorter than its diff:
```python
import functools
import math

import jax
import jax.numpy as jnp
from jax import lax
from jax.experimental import pallas as pl
from jax.experimental.pallas import tpu as pltpu
from jax.sharding import PartitionSpec as P

D = 2048
H = 16
HD = 128
TOK_DEV = 512
RD = 4
LMAX = 128
NB = 8
HALF = TOK_DEV // 2
SEG = 4
COLS = SEG * HD
NT = 256
SCALE = 1.0 / math.sqrt(HD)
SCALE2 = SCALE * math.log2(math.e)
F32 = jnp.float32
BF16 = jnp.bfloat16
MESH = pl.DeviceIdType.MESH
NEG = float(jnp.finfo(jnp.float32).min)


def attend_head(h, qkv, att):
    col = pl.multiple_of(h * HD, HD)
    ones = jnp.ones((TOK_DEV, HD), BF16)
    keys = qkv[1, :, pl.ds(col, HD)]
    values = jnp.concatenate([qkv[2, :, pl.ds(col, HD)], ones], axis=1)
    row = lax.broadcasted_iota(jnp.int32, (HALF, HALF), 0)
    lane = lax.broadcasted_iota(jnp.int32, (HALF, HALF), 1)
    causal = lane <= row
    for part in range(2):
        rows = pl.ds(part * HALF, HALF)
        q = qkv[0, rows, pl.ds(col, HD)]
        blocks = []
        for kb in range(part + 1):
            s = lax.dot_general(
                q,
                keys[kb * HALF : (kb + 1) * HALF],
                (((1,), (1,)), ((), ())),
                preferred_element_type=F32,
            )
            blocks.append(jnp.where(causal, s, NEG) if kb == part else s)
        top = jnp.max(blocks[0], axis=1, keepdims=True)
        for s in blocks[1:]:
            top = jnp.maximum(top, jnp.max(s, axis=1, keepdims=True))
        acc = None
        for kb, s in enumerate(blocks):
            p = jnp.exp2((s - top) * SCALE2).astype(BF16)
            o = jnp.dot(p, values[kb * HALF : (kb + 1) * HALF], preferred_element_type=F32)
            acc = o if acc is None else acc + o
        att[rows, pl.ds(col, HD)] = (acc[:, :HD] / acc[:, HD:]).astype(BF16)


def head_mask():
    row = lax.broadcasted_iota(jnp.int32, (H, D), 0)
    lane = lax.broadcasted_iota(jnp.int32, (H, D), 1)
    return (lane // HD) == row


def pick_row(block, j):
    row = lax.broadcasted_iota(jnp.int32, block.shape, 0)
    return jnp.sum(jnp.where(row == j, block.astype(F32), 0.0), axis=0, keepdims=True)


def pick_lane(block, j):
    lane = lax.broadcasted_iota(jnp.int32, block.shape, 1)
    return jnp.sum(jnp.where(lane == j, block, 0.0), axis=1, keepdims=True)


def kernel(
    na,
    lengths,
    flag,
    cache_slot,
    slot_owner,
    qkv_hbm,
    cache_hbm,
    weight_hbm,
    out_hbm,
    first,
    qkv,
    cache,
    weight,
    att,
    result,
    qg,
    cg,
    sg,
    in_sem,
    out_sem,
    sa,
    ra,
    sb,
    rb,
    sc,
    rc,
    sd,
    rd,
    se,
    re,
    sf,
    rf,
):
    me = lax.axis_index("req")
    a = me // NB
    b = me % NB

    def peer_a(t):
        return lax.rem(a + t, na) * NB + b

    def peer_b(t):
        return a * NB + lax.rem(b + t, NB)

    loads = [pltpu.make_async_copy(qkv_hbm.at[pl.ds(0, 16), :], first, in_sem.at[0])]
    for g in range(H // SEG):
        for part in range(3):
            loads.append(
                pltpu.make_async_copy(
                    qkv_hbm.at[:, pl.ds(part * D + g * COLS, COLS)],
                    qkv.at[part, :, pl.ds(g * COLS, COLS)],
                    in_sem.at[1 + g * 3 + part],
                )
            )
    load_cache = pltpu.make_async_copy(cache_hbm, cache, in_sem.at[13])
    load_weight = pltpu.make_async_copy(weight_hbm, weight, in_sem.at[14])
    for load in loads[:7]:
        load.start()
    load_cache.start()
    for load in loads[7:]:
        load.start()
    load_weight.start()

    barrier = pltpu.get_barrier_semaphore()

    @pl.loop(1, na)
    def _(t):
        pl.semaphore_signal(barrier, inc=1, device_id=(peer_a(t),), device_id_type=MESH)

    @pl.loop(1, NB)
    def _(t):
        pl.semaphore_signal(barrier, inc=1, device_id=(peer_b(t),), device_id_type=MESH)

    loads[0].wait()
    qg[b, a] = first[:, :D].astype(F32)[:RD].astype(BF16)
    pl.semaphore_wait(barrier, na - 1 + NB - 1)

    def copy_a(buf, send, recv, t):
        return pltpu.make_async_remote_copy(
            src_ref=buf.at[b, a],
            dst_ref=buf.at[b, a],
            send_sem=send.at[t - 1],
            recv_sem=recv.at[t - 1],
            device_id=(peer_a(t),),
            device_id_type=MESH,
        )

    def copy_b(buf, send, recv, t):
        return pltpu.make_async_remote_copy(
            src_ref=buf.at[b],
            dst_ref=buf.at[b],
            send_sem=send.at[t - 1],
            recv_sem=recv.at[t - 1],
            device_id=(peer_b(t),),
            device_id_type=MESH,
        )

    def start_a(buf, send, recv):
        @pl.loop(1, na)
        def _(t):
            copy_a(buf, send, recv, t).start()

    def wait_a(buf, send, recv):
        @pl.loop(1, na)
        def _(t):
            copy_a(buf, send, recv, t).wait()

    def start_b(buf, send, recv):
        @pl.loop(1, NB)
        def _(t):
            copy_b(buf, send, recv, t).start()

    def wait_b(buf, send, recv):
        @pl.loop(1, NB)
        def _(t):
            copy_b(buf, send, recv, t).wait()

    def segment(g):
        for load in loads[1 + 3 * g : 4 + 3 * g]:
            load.wait()

        @pl.loop(g * SEG, (g + 1) * SEG)
        def _(h):
            attend_head(h, qkv, att)

    start_a(qg, sa, ra)
    segment(0)
    wait_a(qg, sa, ra)
    start_b(qg, sb, rb)
    segment(1)
    load_cache.wait()
    wait_b(qg, sb, rb)

    own = head_mask()
    row4 = lax.broadcasted_iota(jnp.int32, (RD, D), 0)
    lane_h = lax.broadcasted_iota(jnp.int32, (H, LMAX), 1)
    sums = jnp.zeros((RD, D), F32)
    stats = jnp.zeros((H, 128), F32)
    for s in range(RD):
        owner = slot_owner[s]
        device = owner // RD
        block = qg[device % NB, device // NB]
        q = pick_row(block, owner % RD)
        q_heads = jnp.where(own, q, 0.0).astype(BF16)
        scores = lax.dot_general(
            q_heads, cache[s, :, :D], (((1,), (1,)), ((), ())), preferred_element_type=F32
        )
        scores = jnp.where(lane_h < lengths[s], scores, NEG)
        top = jnp.max(scores, axis=1, keepdims=True)
        p = jnp.where(lane_h < lengths[s], jnp.exp2((scores - top) * SCALE2), 0.0)
        total = jnp.sum(p, axis=1, keepdims=True)
        o = jnp.dot(p.astype(BF16), cache[s, :, D:], preferred_element_type=F32)
        o = jnp.sum(jnp.where(own, o / total, 0.0), axis=0, keepdims=True)
        sums = jnp.where(row4 == s, o, sums)
        stats = jnp.where(lane_h == s, top * SCALE, jnp.where(lane_h == RD + s, total, stats))
    cg[b, a] = sums.astype(BF16)
    sg[b, a] = stats

    start_a(cg, sc, rc)
    start_a(sg, sd, rd)
    segment(2)
    wait_a(cg, sc, rc)
    wait_a(sg, sd, rd)
    start_b(cg, se, re)
    start_b(sg, sf, rf)
    segment(3)
    load_weight.wait()
    is_prefill = flag[0] == 1

    def project(part):
        @pl.loop(0, D // NT)
        def _(n):
            cols = pl.ds(pl.multiple_of(n * NT, NT), NT)
            rows = pl.ds(part * HALF, HALF)
            acc = jnp.dot(att[rows, :], weight[:, cols], preferred_element_type=F32)
            if part == 1:
                acc = jnp.where(is_prefill, acc, 0.0)
            result[rows, cols] = acc.astype(BF16)

        return pltpu.make_async_copy(
            result.at[pl.ds(part * HALF, HALF), :],
            out_hbm.at[pl.ds(part * HALF, HALF), :],
            out_sem.at[part],
        )

    lower = project(1)
    lower.start()
    wait_b(cg, se, re)
    wait_b(sg, sf, rf)

    row16 = lax.broadcasted_iota(jnp.int32, (H, D), 0)
    decoded = jnp.zeros((H, D), F32)
    for j in range(RD):
        slot = cache_slot[j]
        device = slot // RD
        co = pick_row(cg[device % NB, device // NB], slot % RD)
        stat = sg[device % NB, device // NB]
        cm = pick_lane(stat, slot % RD)
        cl = pick_lane(stat, RD + slot % RD)
        mine = first[...].astype(F32)[j : j + 1]
        product = mine[:, :D] * mine[:, D : 2 * D]
        ns = jnp.sum(jnp.where(own, product, 0.0), axis=1, keepdims=True) * SCALE
        joint = jnp.maximum(cm, ns)
        wc = cl * jnp.exp(cm - joint)
        wo = jnp.exp(ns - joint)
        mixed = (co * wc + mine[:, 2 * D :] * wo) / (wc + wo)
        decoded = jnp.where(
            row16 == j, jnp.sum(jnp.where(own, mixed, 0.0), axis=0, keepdims=True), decoded
        )
    kept = jnp.where(is_prefill, att[pl.ds(0, H), :].astype(F32), decoded)
    att[pl.ds(0, H), :] = kept.astype(BF16)
    rest = att[pl.ds(H, HALF - H), :]
    att[pl.ds(H, HALF - H), :] = jnp.where(is_prefill, rest, jnp.zeros_like(rest))
    upper = project(0)
    upper.start()
    lower.wait()
    upper.wait()


def local(hidden_in, qkv, cache, lengths, prefill_flag, cache_slot, slot_owner, out_weight, n):
    na = n // NB
    smem = pl.BlockSpec(memory_space=pltpu.SMEM)
    hbm = pl.BlockSpec(memory_space=pl.ANY)
    dma = pltpu.SemaphoreType.DMA
    projected = pl.pallas_call(
        functools.partial(kernel, na),
        out_shape=jax.ShapeDtypeStruct((TOK_DEV, D), BF16),
        in_specs=[smem] * 4 + [hbm] * 3,
        out_specs=hbm,
        scratch_shapes=[
            pltpu.VMEM((16, 3 * D), BF16),
            pltpu.VMEM((3, TOK_DEV, D), BF16),
            pltpu.VMEM((RD, LMAX, 2 * D), BF16),
            pltpu.VMEM((D, D), BF16),
            pltpu.VMEM((TOK_DEV, D), BF16),
            pltpu.VMEM((TOK_DEV, D), BF16),
            pltpu.VMEM((NB, na, RD, D), BF16),
            pltpu.VMEM((NB, na, RD, D), BF16),
            pltpu.VMEM((NB, na, H, 128), F32),
            dma((15,)),
            dma((2,)),
            dma((na - 1,)),
            dma((na - 1,)),
            dma((NB - 1,)),
            dma((NB - 1,)),
            dma((na - 1,)),
            dma((na - 1,)),
            dma((na - 1,)),
            dma((na - 1,)),
            dma((NB - 1,)),
            dma((NB - 1,)),
            dma((NB - 1,)),
            dma((NB - 1,)),
        ],
        compiler_params=pltpu.CompilerParams(
            collective_id=0, has_side_effects=True, vmem_limit_bytes=48 * 1024 * 1024
        ),
    )(lengths, prefill_flag, cache_slot, slot_owner, qkv, cache, out_weight)
    summed = hidden_in.astype(F32) + projected.astype(F32)
    return summed.astype(BF16)


def solution(mesh):
    placed = (
        P("req", None),
        P("req", None),
        P("req", None, None),
        P("req"),
        P("req"),
        P("req"),
        P("req"),
        P(),
    )
    return jax.shard_map(
        functools.partial(local, n=mesh.shape["req"]),
        mesh=mesh,
        in_specs=placed,
        out_specs=P("req", None),
        check_vma=False,
    )
```

time: 232 us -> 43.1 us (0.19)
  blocking collectives: 157 us -> 0 us
  Pallas kernels: 0 us -> 38.1 us
  matrix products: 30.8 us -> 0 us
  local copies, waits for them, and re-layouts: 24.7 us -> 1.96 us
  other arithmetic: 17.4 us -> 2.14 us
    all_gather x4 -> x0, blocking collectives: 157 us -> none  [the longest x1 44.6 us: local(): every_query = lax.all_gather(request_rows[:, :D], 'req', axis=0, tiled=True)]
    pallas_call x0 -> x1, Pallas kernels: none -> 38.1 us  [local(): pl.pallas_call(functools.partial(kernel, na), out_shape=jax.ShapeDtypeStr...]
    dot_general x5 -> x0, matrix products: 30.8 us -> none  [the longest x1 10.9 us: prefill_attention(): jnp.einsum('hqk,khd->qhd', expon.astype(jnp.bfloat16), values_new, prefer...]
    reduce_sum x2 -> x0, other arithmetic: 9.23 us -> none  [the longest x1 9.15 us: prefill_attention(): totals = jnp.sum(expon, axis=-1)]
    another operation x1 -> x0, local copies, waits for them, and re-layouts: 8.85 us -> none
    slice x1 -> x0, local copies, waits for them, and re-layouts: 4.58 us -> none  [prefill_attention(): keys_new = block[:, D:2 * D].reshape(TOK_DEV, H, HD)]
    unnamed x8, local copies, waits for them, and re-layouts: 5.91 us -> 1.96 us
    reshape x2 -> x0, local copies, waits for them, and re-layouts: 3.06 us -> none  [the longest x1 3.03 us: holder_partial(): cache_keys = cache[:, :, :D].reshape(RD, LMAX, H, HD)]
where the time goes in v1:
time: 43.1 us; the launch traced here: 42.9 us
  Pallas kernels  38.1 us (88%)
  other arithmetic  2.14 us (5%)
  local copies, waits for them, and re-layouts  1.96 us (5%)
  between operations  0.68 us (2%)
    pallas_call x1, Pallas kernels, local(): pl.pallas_call(functools.partial(kernel, na), out_shape=jax.ShapeDtypeStr...  38.1 us
    convert_element_type x1, other arithmetic, local(): return summed.astype(BF16)  2.14 us
    unnamed x8, local copies, waits for them, and re-layouts  1.96 us

profile of v1, /device:TPU:0, one launch (start us, length us, event | category | flops | bytes accessed | tf_op | source)
XLA Modules:
  0.0 42.9 jit_solution(18082311454565972372)
XLA Ops:
  0.7 0.0 copy-start
  0.7 0.6 %copy-done = s32[4]{0:T(128)S(1)} copy-done((s32[4]{0:T(128)S(1)}, s32[4]{0:T(128)}, u32[]{:S(2)}) %copy-start) | copy-done | bytes 40
  1.3 0.0 copy-start.1
  1.3 0.7 %copy-done.1 = s32[4]{0:T(128)S(1)} copy-done((s32[4]{0:T(128)S(1)}, s32[4]{0:T(128)}, u32[]{:S(2)}) %copy-start.1) | copy-done | bytes 40
  2.0 0.0 copy-start.2
  2.0 0.7 %copy-done.2 = s32[4]{0:T(128)S(1)} copy-done((s32[4]{0:T(128)S(1)}, s32[4]{0:T(128)}, u32[]{:S(2)}) %copy-start.2) | copy-done | bytes 40
  2.6 0.0 copy-start.3
  2.6 38.1 %shard_map.82 = bf16[512,2048]{1,0:T(8,128)(2,1)S(1)} custom-call(s32[4]{0:T(128)S(1)} %copy-done, s32[1]{0:T(128)S(6)} %copy.9.flag, s32[4]{0:T(128)S(1)} %copy-done.1, s32[4]{0:T(128)S(1)} %copy-done.2, bf16[512,6144]{1,0:T(8,128)(2,1)} %qkv_hbm.1, bf16[4,128,4096]{2,1,0:T(8,128)(2,1)} %cache_hbm.1, bf16[2048,2048]{1,0:T(8,128)(2,1)} %weight_hbm.1), custom_call_target="tpu_custom_call" | custom-call | tf_op jit(solution)/shard_map/pallas_call | solution.py:301
  40.7 0.0 copy-done.3
  40.7 2.1 %add_convert_fusion = bf16[512,2048]{1,0:T(8,128)(2,1)} fusion(bf16[512,2048]{1,0:T(8,128)(2,1)S(1)} %shard_map.82, bf16[512,2048]{1,0:T(8,128)(2,1)S(1)} %copy-done.3), kind=kLoop, calls=%fused_computation | loop fusion | flops 4194304 | bytes 6291456 | tf_op jit(solution)/shard_map/convert_element_type | solution.py:336
Async XLA Ops:
  0.7 0.7 %copy-start = (s32[4]{0:T(128)S(1)}, s32[4]{0:T(128)}, u32[]{:S(2)}) copy-start(s32[4]{0:T(128)} %lengths.1) | copy-start | bytes 52
  1.3 0.7 %copy-start.1 = (s32[4]{0:T(128)S(1)}, s32[4]{0:T(128)}, u32[]{:S(2)}) copy-start(s32[4]{0:T(128)} %cache_slot.1) | copy-start | bytes 52
  2.0 0.7 %copy-start.2 = (s32[4]{0:T(128)S(1)}, s32[4]{0:T(128)}, u32[]{:S(2)}) copy-start(s32[4]{0:T(128)} %slot_owner.1) | copy-start | bytes 52
  2.6 38.1 %copy-start.3 = (bf16[512,2048]{1,0:T(8,128)(2,1)S(1)}, bf16[512,2048]{1,0:T(8,128)(2,1)}, u32[]{:S(2)}) copy-start(bf16[512,2048]{1,0:T(8,128)(2,1)} %param.8) | copy-start | bytes 6291460

commit v2 on v1

v2 whole, which is shorter than its diff:
```python
import functools
import math

import jax
import jax.numpy as jnp
from jax import lax
from jax.experimental import pallas as pl
from jax.experimental.pallas import tpu as pltpu
from jax.sharding import PartitionSpec as P

D = 2048
H = 16
HD = 128
TOK_DEV = 512
RD = 4
LMAX = 128
NB = 8
HALF = TOK_DEV // 2
CUTS = ((0, 4), (4, 8), (8, 16))
SEG = 4
TAIL = 128
NT = 1024
EXT = D + HD
MARK = 96
SCALE = 1.0 / math.sqrt(HD)
SCALE2 = SCALE * math.log2(math.e)
F32 = jnp.float32
BF16 = jnp.bfloat16
MESH = pl.DeviceIdType.MESH
NEG = float(jnp.finfo(jnp.float32).min)


def score(x, y):
    return lax.dot_general(x, y, (((1,), (1,)), ((), ())), preferred_element_type=F32)


def attend_head(h, qkv, att):
    col = pl.multiple_of(h * HD, HD)
    q = qkv[0, :, pl.ds(col, HD)]
    keys = qkv[1, :, pl.ds(col, HD)]
    ones = jnp.ones((TOK_DEV, HD), BF16)
    values = jnp.concatenate([qkv[2, :, pl.ds(col, HD)], ones], axis=1)
    row = lax.broadcasted_iota(jnp.int32, (HALF, HALF), 0)
    lane = lax.broadcasted_iota(jnp.int32, (HALF, HALF), 1)
    causal = lane <= row
    s_first = score(q, keys[:HALF])
    s_last = jnp.where(causal, score(q[HALF:], keys[HALF:]), NEG)
    s_upper = jnp.where(causal, s_first[:HALF], NEG)
    s_lower = s_first[HALF:]
    top_upper = jnp.max(s_upper, axis=1, keepdims=True)
    top_lower = jnp.max(jnp.maximum(s_lower, s_last), axis=1, keepdims=True)
    p_upper = jnp.exp2((s_upper - top_upper) * SCALE2).astype(BF16)
    p_lower = jnp.exp2((s_lower - top_lower) * SCALE2).astype(BF16)
    p_last = jnp.exp2((s_last - top_lower) * SCALE2).astype(BF16)
    lower = jnp.dot(
        jnp.concatenate([p_lower, p_last], axis=1), values, preferred_element_type=F32
    )
    upper = jnp.dot(p_upper, values[:HALF], preferred_element_type=F32)
    att[pl.ds(0, HALF), pl.ds(col, HD)] = (upper[:, :HD] / upper[:, HD:]).astype(BF16)
    att[pl.ds(HALF, HALF), pl.ds(col, HD)] = (lower[:, :HD] / lower[:, HD:]).astype(BF16)


def head_mask():
    row = lax.broadcasted_iota(jnp.int32, (H, D), 0)
    lane = lax.broadcasted_iota(jnp.int32, (H, D), 1)
    return (lane // HD) == row


def pick_row(block, j):
    row = lax.broadcasted_iota(jnp.int32, block.shape, 0)
    return jnp.sum(jnp.where(row == j, block.astype(F32), 0.0), axis=0, keepdims=True)


def pick_marked(block, place):
    block = block.astype(F32)
    lane = lax.broadcasted_iota(jnp.int32, (2, HD), 1)
    mark = jnp.sum(jnp.where(lane == MARK, block[:, D:], 0.0), axis=1, keepdims=True)
    wanted = mark == place.astype(F32)
    return jnp.sum(jnp.where(wanted, block, 0.0), axis=0, keepdims=True)


def split3(x):
    pieces = []
    for _ in range(3):
        piece = x.astype(BF16).astype(F32)
        pieces.append(piece)
        x = x - piece
    return pieces


def first_two(far):
    one = jnp.int32(-1)
    two = jnp.int32(-1)
    for j in reversed(range(RD)):
        two = jnp.where(far[j], one, two)
        one = jnp.where(far[j], jnp.int32(j), one)
    return one, two


def message(rows, places):
    lane = lax.broadcasted_iota(jnp.int32, (1, EXT), 1)
    row = lax.broadcasted_iota(jnp.int32, (2, EXT), 0)
    marked = [
        jnp.where(lane == D + MARK, place.astype(F32), x) for x, place in zip(rows, places)
    ]
    return jnp.where(row == 0, marked[0], marked[1]).astype(BF16)


def partial(q, slot, cache, lengths, own):
    valid = lax.broadcasted_iota(jnp.int32, (H, LMAX), 1) < lengths[slot]
    q_heads = jnp.where(own, q, 0.0).astype(BF16)
    scores = jnp.where(valid, score(q_heads, cache[slot, :, pl.ds(0, D)]), NEG)
    top = jnp.max(scores, axis=1, keepdims=True)
    p = jnp.where(valid, jnp.exp2((scores - top) * SCALE2), 0.0)
    total = jnp.sum(p, axis=1, keepdims=True)
    o = jnp.dot(p.astype(BF16), cache[slot, :, pl.ds(D, D)], preferred_element_type=F32)
    o = jnp.sum(jnp.where(own, o / total, 0.0), axis=0, keepdims=True)
    row = lax.broadcasted_iota(jnp.int32, (H, HD), 0)
    lane = lax.broadcasted_iota(jnp.int32, (H, HD), 1)
    stats = jnp.zeros((H, HD), F32)
    for k, piece in enumerate(split3(top * SCALE) + split3(total)):
        stats = jnp.where(lane == row + k * H, piece, stats)
    return jnp.concatenate([o, jnp.sum(stats, axis=0, keepdims=True)], axis=1)


def kernel(
    na,
    lengths_hbm,
    flag_hbm,
    cache_slot_hbm,
    slot_owner_hbm,
    hidden_hbm,
    qkv_hbm,
    cache_hbm,
    weight_hbm,
    out_any,
    lengths,
    flag,
    cache_slot,
    slot_owner,
    first,
    hidden,
    qkv,
    cache,
    weight,
    att,
    out,
    local_part,
    qg,
    cg,
    in_sem,
    out_sem,
    sa,
    ra,
    sb,
    rb,
    sc,
    rc,
    sd,
    rd,
):
    me = lax.axis_index("req")
    a = me // NB
    b = me % NB

    def peer_a(t):
        return lax.rem(a + t, na) * NB + b

    def peer_b(t):
        return a * NB + lax.rem(b + t, NB)

    small = [
        pltpu.make_async_copy(src, dst, in_sem.at[i])
        for i, (src, dst) in enumerate(
            [
                (cache_slot_hbm, cache_slot),
                (qkv_hbm.at[pl.ds(0, 16), :], first),
                (lengths_hbm, lengths),
                (slot_owner_hbm, slot_owner),
                (flag_hbm, flag),
            ]
        )
    ]
    load_cache = pltpu.make_async_copy(cache_hbm, cache, in_sem.at[5])
    load_weight = pltpu.make_async_copy(weight_hbm, weight, in_sem.at[6])
    load_hidden = pltpu.make_async_copy(hidden_hbm, hidden, in_sem.at[7])
    loads = []
    for start, stop in CUTS:
        for part in range(3):
            loads.append(
                pltpu.make_async_copy(
                    qkv_hbm.at[:, pl.ds(part * D + start * HD, (stop - start) * HD)],
                    qkv.at[part, :, pl.ds(start * HD, (stop - start) * HD)],
                    in_sem.at[8 + len(loads)],
                )
            )
    for load in small:
        load.start()

    barrier = pltpu.get_barrier_semaphore()

    @pl.loop(1, na)
    def _(t):
        pl.semaphore_signal(barrier, inc=1, device_id=(peer_a(t),), device_id_type=MESH)

    @pl.loop(1, NB)
    def _(t):
        pl.semaphore_signal(barrier, inc=1, device_id=(peer_b(t),), device_id_type=MESH)

    load_cache.start()
    for load in loads:
        load.start()
    load_weight.start()
    load_hidden.start()

    def copy_a(buf, send, recv, t):
        return pltpu.make_async_remote_copy(
            src_ref=buf.at[b, a],
            dst_ref=buf.at[b, a],
            send_sem=send.at[t - 1],
            recv_sem=recv.at[t - 1],
            device_id=(peer_a(t),),
            device_id_type=MESH,
        )

    def copy_b(buf, send, recv, t):
        return pltpu.make_async_remote_copy(
            src_ref=buf.at[b],
            dst_ref=buf.at[b],
            send_sem=send.at[t - 1],
            recv_sem=recv.at[t - 1],
            device_id=(peer_b(t),),
            device_id_type=MESH,
        )

    def start_a(buf, send, recv):
        @pl.loop(1, na)
        def _(t):
            copy_a(buf, send, recv, t).start()

    def wait_a(buf, send, recv):
        @pl.loop(1, na)
        def _(t):
            copy_a(buf, send, recv, t).wait()

    def start_b(buf, send, recv):
        @pl.loop(1, NB)
        def _(t):
            copy_b(buf, send, recv, t).start()

    def wait_b(buf, send, recv):
        @pl.loop(1, NB)
        def _(t):
            copy_b(buf, send, recv, t).wait()

    def segment(g):
        for load in loads[3 * g : 3 * g + 3]:
            load.wait()
        start, stop = CUTS[g]

        @pl.loop(start // SEG, stop // SEG)
        def _(i):
            for u in range(SEG):
                attend_head(i * SEG + u, qkv, att)

    for load in small:
        load.wait()
    own = head_mask()
    mine = first[...].astype(F32)[:8]
    places = first_two([cache_slot[j] // RD != me for j in range(RD)])
    no_stats = jnp.zeros((1, HD), F32)
    qg[b, a] = message(
        [jnp.concatenate([pick_row(mine[:, :D], j), no_stats], axis=1) for j in places], places
    )
    pl.semaphore_wait(barrier, na - 1 + NB - 1)
    start_a(qg, sa, ra)

    load_cache.wait()
    row8 = lax.broadcasted_iota(jnp.int32, (8, EXT), 0)
    held = jnp.zeros((8, EXT), F32)
    for j in range(RD):
        part = partial(mine[j : j + 1, :D], cache_slot[j] % RD, cache, lengths, own)
        held = jnp.where(row8 == j, part, held)
    local_part[...] = held

    wait_a(qg, sa, ra)
    start_b(qg, sb, rb)
    segment(0)
    wait_b(qg, sb, rb)

    places = first_two([slot_owner[s] // RD != me for s in range(RD)])
    rows = []
    for place in places:
        slot = jnp.maximum(place, 0)
        owner = slot_owner[slot]
        device = owner // RD
        q = pick_marked(qg[device % NB, device // NB], owner % RD)
        rows.append(partial(q[:, :D], slot, cache, lengths, own))
    cg[b, a] = message(rows, places)

    start_a(cg, sc, rc)
    segment(1)
    wait_a(cg, sc, rc)
    start_b(cg, sd, rd)
    segment(2)
    load_weight.wait()
    load_hidden.wait()
    is_prefill = flag[0] == 1

    def project(start, stop):
        @pl.loop(0, D // NT)
        def _(n):
            cols = pl.ds(pl.multiple_of(n * NT, NT), NT)
            rows = pl.ds(start, stop - start)
            acc = jnp.dot(att[rows, :], weight[:, cols], preferred_element_type=F32)
            if start >= H:
                acc = jnp.where(is_prefill, acc, 0.0)
            projected = acc.astype(BF16).astype(F32)
            out[rows, cols] = (hidden[rows, cols].astype(F32) + projected).astype(BF16)

        rows = pl.ds(start, stop - start)
        store = pltpu.make_async_copy(
            out.at[rows, :], out_any.at[rows, :], out_sem.at[int(start == 0)]
        )
        store.start()
        return store

    store_lower = project(TAIL, TOK_DEV)
    wait_b(cg, sd, rd)

    row16 = lax.broadcasted_iota(jnp.int32, (H, D), 0)
    row_h = lax.broadcasted_iota(jnp.int32, (H, HD), 0)
    lane_h = lax.broadcasted_iota(jnp.int32, (H, HD), 1)
    diagonal = lane_h % H == row_h
    is_max = jnp.logical_and(diagonal, lane_h < 3 * H)
    is_total = jnp.logical_and(
        diagonal, jnp.logical_and(lane_h >= 3 * H, lane_h < 6 * H)
    )
    decoded = jnp.zeros((H, D), F32)
    for j in range(RD):
        slot = cache_slot[j]
        device = slot // RD
        far = pick_marked(cg[device % NB, device // NB], slot % RD)
        part = jnp.where(device == me, local_part[j : j + 1, :], far)
        co = part[:, :D]
        cm = jnp.sum(jnp.where(is_max, part[:, D:], 0.0), axis=1, keepdims=True)
        cl = jnp.sum(jnp.where(is_total, part[:, D:], 0.0), axis=1, keepdims=True)
        row = mine[j : j + 1]
        product = row[:, :D] * row[:, D : 2 * D]
        ns = jnp.sum(jnp.where(own, product, 0.0), axis=1, keepdims=True) * SCALE
        joint = jnp.maximum(cm, ns)
        wc = cl * jnp.exp(cm - joint)
        wo = jnp.exp(ns - joint)
        mixed = co * (wc / (wc + wo)) + row[:, 2 * D :] * (wo / (wc + wo))
        decoded = jnp.where(
            row16 == j, jnp.sum(jnp.where(own, mixed, 0.0), axis=0, keepdims=True), decoded
        )
    kept = jnp.where(is_prefill, att[pl.ds(0, H), :].astype(F32), decoded)
    att[pl.ds(0, H), :] = kept.astype(BF16)
    rest = att[pl.ds(H, TAIL - H), :]
    att[pl.ds(H, TAIL - H), :] = jnp.where(is_prefill, rest, jnp.zeros_like(rest))
    store_upper = project(0, TAIL)
    store_lower.wait()
    store_upper.wait()


def local(hidden_in, qkv, cache, lengths, prefill_flag, cache_slot, slot_owner, out_weight, n):
    na = n // NB
    hbm = pl.BlockSpec(memory_space=pltpu.HBM)
    dma = pltpu.SemaphoreType.DMA
    return pl.pallas_call(
        functools.partial(kernel, na),
        out_shape=jax.ShapeDtypeStruct((TOK_DEV, D), BF16),
        in_specs=[hbm] * 8,
        out_specs=pl.BlockSpec(memory_space=pl.ANY),
        scratch_shapes=[
            pltpu.SMEM((RD,), jnp.int32),
            pltpu.SMEM((1,), jnp.int32),
            pltpu.SMEM((RD,), jnp.int32),
            pltpu.SMEM((RD,), jnp.int32),
            pltpu.VMEM((16, 3 * D), BF16),
            pltpu.VMEM((TOK_DEV, D), BF16),
            pltpu.VMEM((3, TOK_DEV, D), BF16),
            pltpu.VMEM((RD, LMAX, 2 * D), BF16),
            pltpu.VMEM((D, D), BF16),
            pltpu.VMEM((TOK_DEV, D), BF16),
            pltpu.VMEM((TOK_DEV, D), BF16),
            pltpu.VMEM((8, EXT), F32),
            pltpu.VMEM((NB, na, 2, EXT), BF16),
            pltpu.VMEM((NB, na, 2, EXT), BF16),
            dma((8 + 3 * len(CUTS),)),
            dma((2,)),
            dma((na - 1,)),
            dma((na - 1,)),
            dma((NB - 1,)),
            dma((NB - 1,)),
            dma((na - 1,)),
            dma((na - 1,)),
            dma((NB - 1,)),
            dma((NB - 1,)),
        ],
        compiler_params=pltpu.CompilerParams(
            collective_id=0, has_side_effects=True, vmem_limit_bytes=61 * 1024 * 1024
        ),
    )(
        lengths,
        prefill_flag,
        cache_slot,
        slot_owner,
        hidden_in,
        qkv,
        cache,
        out_weight,
    )


def solution(mesh):
    placed = (
        P("req", None),
        P("req", None),
        P("req", None, None),
        P("req"),
        P("req"),
        P("req"),
        P("req"),
        P(),
    )
    return jax.shard_map(
        functools.partial(local, n=mesh.shape["req"]),
        mesh=mesh,
        in_specs=placed,
        out_specs=P("req", None),
        check_vma=False,
    )
```

time: 43.1 us -> 32.6 us (0.76)
  Pallas kernels: 38.1 us -> 28.6 us
  other arithmetic: 2.14 us -> 0 us
  local copies, waits for them, and re-layouts: 1.96 us -> 3.16 us
    pallas_call x1, Pallas kernels: 38.1 us -> 28.6 us  [local(): pl.pallas_call(functools.partial(kernel, na), out_shape=jax.ShapeDtypeStr...]
    convert_element_type x1 -> x0, other arithmetic: 2.14 us -> none  [local(): return summed.astype(BF16)]
    unnamed x8 -> x1, local copies, waits for them, and re-layouts: 1.96 us -> 3.16 us
where the time goes in v2:
time: 32.6 us; the launch traced here: 32.4 us
  Pallas kernels  28.6 us (88%)
  local copies, waits for them, and re-layouts  3.16 us (10%)
  between operations  0.66 us (2%)
    pallas_call x1, Pallas kernels, local(): pl.pallas_call(functools.partial(kernel, na), out_shape=jax.ShapeDtypeStr...  28.6 us
    unnamed x1, local copies, waits for them, and re-layouts  3.16 us

profile of v2, /device:TPU:0, one launch (start us, length us, event | category | flops | bytes accessed | tf_op | source)
XLA Modules:
  0.0 32.4 jit_solution(6317753565098297801)
XLA Ops:
  0.7 28.6 %shard_map.82 = bf16[512,2048]{1,0:T(8,128)(2,1)} custom-call(s32[4]{0:T(128)} %lengths_hbm.1, s32[1]{0:T(128)S(6)} %copy.10.flag_hbm, s32[4]{0:T(128)} %cache_slot_hbm.1, s32[4]{0:T(128)} %slot_owner_hbm.1, bf16[512,2048]{1,0:T(8,128)(2,1)} %hidden_hbm.1, bf16[512,6144]{1,0:T(8,128)(2,1)} %qkv_hbm.1, bf16[4,128,4096]{2,1,0:T(8,128)(2,1)} %cache_hbm.1, ...), custom_call_target="tpu_custom_call" | custom-call | tf_op jit(solution)/shard_map/pallas_call | solution.py:371
  29.2 3.2 %copy.11 = bf16[512,2048]{1,0:T(8,128)(2,1)} copy(bf16[512,2048]{1,0:T(8,128)(2,1)} %shard_map.82) | data formatting | bytes 4194304

commit v3 on v2

--- a/solution.py
+++ b/solution.py
@@ -16,8 +16,7 @@
 LMAX = 128
 NB = 8
 HALF = TOK_DEV // 2
-CUTS = ((0, 4), (4, 8), (8, 16))
-SEG = 4
+CUTS = ((0, 6), (6, 12), (12, 16))
 TAIL = 128
 NT = 1024
 EXT = D + HD
@@ -35,7 +34,7 @@
 
 
 def attend_head(h, qkv, att):
-    col = pl.multiple_of(h * HD, HD)
+    col = h * HD
     q = qkv[0, :, pl.ds(col, HD)]
     keys = qkv[1, :, pl.ds(col, HD)]
     ones = jnp.ones((TOK_DEV, HD), BF16)
@@ -106,8 +105,8 @@
     return jnp.where(row == 0, marked[0], marked[1]).astype(BF16)
 
 
-def partial(q, slot, cache, lengths, own):
-    valid = lax.broadcasted_iota(jnp.int32, (H, LMAX), 1) < lengths[slot]
+def partial(q, slot, cache, table, own):
+    valid = lax.broadcasted_iota(jnp.int32, (H, LMAX), 1) < table[slot]
     q_heads = jnp.where(own, q, 0.0).astype(BF16)
     scores = jnp.where(valid, score(q_heads, cache[slot, :, pl.ds(0, D)]), NEG)
     top = jnp.max(scores, axis=1, keepdims=True)
@@ -125,21 +124,13 @@
 
 def kernel(
     na,
-    lengths_hbm,
-    flag_hbm,
-    cache_slot_hbm,
-    slot_owner_hbm,
-    hidden_hbm,
+    table_hbm,
     qkv_hbm,
     cache_hbm,
     weight_hbm,
     out_any,
-    lengths,
-    flag,
-    cache_slot,
-    slot_owner,
+    table,
     first,
-    hidden,
     qkv,
     cache,
     weight,
@@ -173,17 +164,13 @@
         pltpu.make_async_copy(src, dst, in_sem.at[i])
         for i, (src, dst) in enumerate(
             [
-                (cache_slot_hbm, cache_slot),
+                (table_hbm, table),
                 (qkv_hbm.at[pl.ds(0, 16), :], first),
-                (lengths_hbm, lengths),
-                (slot_owner_hbm, slot_owner),
-                (flag_hbm, flag),
             ]
         )
     ]
     load_cache = pltpu.make_async_copy(cache_hbm, cache, in_sem.at[5])
     load_weight = pltpu.make_async_copy(weight_hbm, weight, in_sem.at[6])
-    load_hidden = pltpu.make_async_copy(hidden_hbm, hidden, in_sem.at[7])
     loads = []
     for start, stop in CUTS:
         for part in range(3):
@@ -211,7 +198,6 @@
     for load in loads:
         load.start()
     load_weight.start()
-    load_hidden.start()
 
     def copy_a(buf, send, recv, t):
         return pltpu.make_async_remote_copy(
@@ -258,16 +244,14 @@
             load.wait()
         start, stop = CUTS[g]
 
-        @pl.loop(start // SEG, stop // SEG)
-        def _(i):
-            for u in range(SEG):
-                attend_head(i * SEG + u, qkv, att)
+        for h in range(start, stop):
+            attend_head(h, qkv, att)
 
     for load in small:
         load.wait()
     own = head_mask()
     mine = first[...].astype(F32)[:8]
-    places = first_two([cache_slot[j] // RD != me for j in range(RD)])
+    places = first_two([table[RD + j] // RD != me for j in range(RD)])
     no_stats = jnp.zeros((1, HD), F32)
     qg[b, a] = message(
         [jnp.concatenate([pick_row(mine[:, :D], j), no_stats], axis=1) for j in places], places
@@ -279,7 +263,7 @@
     row8 = lax.broadcasted_iota(jnp.int32, (8, EXT), 0)
     held = jnp.zeros((8, EXT), F32)
     for j in range(RD):
-        part = partial(mine[j : j + 1, :D], cache_slot[j] % RD, cache, lengths, own)
+        part = partial(mine[j : j + 1, :D], table[RD + j] % RD, cache, table, own)
         held = jnp.where(row8 == j, part, held)
     local_part[...] = held
 
@@ -288,14 +272,14 @@
     segment(0)
     wait_b(qg, sb, rb)
 
-    places = first_two([slot_owner[s] // RD != me for s in range(RD)])
+    places = first_two([table[2 * RD + s] // RD != me for s in range(RD)])
     rows = []
     for place in places:
         slot = jnp.maximum(place, 0)
-        owner = slot_owner[slot]
+        owner = table[2 * RD + slot]
         device = owner // RD
         q = pick_marked(qg[device % NB, device // NB], owner % RD)
-        rows.append(partial(q[:, :D], slot, cache, lengths, own))
+        rows.append(partial(q[:, :D], slot, cache, table, own))
     cg[b, a] = message(rows, places)
 
     start_a(cg, sc, rc)
@@ -304,8 +288,7 @@
     start_b(cg, sd, rd)
     segment(2)
     load_weight.wait()
-    load_hidden.wait()
-    is_prefill = flag[0] == 1
+    is_prefill = table[3 * RD] == 1
 
     def project(start, stop):
         @pl.loop(0, D // NT)
@@ -315,8 +298,7 @@
             acc = jnp.dot(att[rows, :], weight[:, cols], preferred_element_type=F32)
             if start >= H:
                 acc = jnp.where(is_prefill, acc, 0.0)
-            projected = acc.astype(BF16).astype(F32)
-            out[rows, cols] = (hidden[rows, cols].astype(F32) + projected).astype(BF16)
+            out[rows, cols] = acc.astype(BF16)
 
         rows = pl.ds(start, stop - start)
         store = pltpu.make_async_copy(
@@ -324,6 +306,13 @@
         )
         store.start()
         return store
+
+    own_scores = []
+    for j in range(RD):
+        product = mine[j : j + 1, :D] * mine[j : j + 1, D : 2 * D]
+        own_scores.append(
+            jnp.sum(jnp.where(own, product, 0.0), axis=1, keepdims=True) * SCALE
+        )
 
     store_lower = project(TAIL, TOK_DEV)
     wait_b(cg, sd, rd)
@@ -338,7 +327,7 @@
     )
     decoded = jnp.zeros((H, D), F32)
     for j in range(RD):
-        slot = cache_slot[j]
+        slot = table[RD + j]
         device = slot // RD
         far = pick_marked(cg[device % NB, device // NB], slot % RD)
         part = jnp.where(device == me, local_part[j : j + 1, :], far)
@@ -346,8 +335,7 @@
         cm = jnp.sum(jnp.where(is_max, part[:, D:], 0.0), axis=1, keepdims=True)
         cl = jnp.sum(jnp.where(is_total, part[:, D:], 0.0), axis=1, keepdims=True)
         row = mine[j : j + 1]
-        product = row[:, :D] * row[:, D : 2 * D]
-        ns = jnp.sum(jnp.where(own, product, 0.0), axis=1, keepdims=True) * SCALE
+        ns = own_scores[j]
         joint = jnp.maximum(cm, ns)
         wc = cl * jnp.exp(cm - joint)
         wo = jnp.exp(ns - joint)
@@ -368,18 +356,15 @@
     na = n // NB
     hbm = pl.BlockSpec(memory_space=pltpu.HBM)
     dma = pltpu.SemaphoreType.DMA
-    return pl.pallas_call(
+    table = jnp.concatenate([lengths, cache_slot, slot_owner, prefill_flag])
+    projected = pl.pallas_call(
         functools.partial(kernel, na),
         out_shape=jax.ShapeDtypeStruct((TOK_DEV, D), BF16),
-        in_specs=[hbm] * 8,
+        in_specs=[hbm] * 4,
         out_specs=pl.BlockSpec(memory_space=pl.ANY),
         scratch_shapes=[
-            pltpu.SMEM((RD,), jnp.int32),
-            pltpu.SMEM((1,), jnp.int32),
-            pltpu.SMEM((RD,), jnp.int32),
-            pltpu.SMEM((RD,), jnp.int32),
+            pltpu.SMEM((3 * RD + 1,), jnp.int32),
             pltpu.VMEM((16, 3 * D), BF16),
-            pltpu.VMEM((TOK_DEV, D), BF16),
             pltpu.VMEM((3, TOK_DEV, D), BF16),
             pltpu.VMEM((RD, LMAX, 2 * D), BF16),
             pltpu.VMEM((D, D), BF16),
@@ -400,18 +385,15 @@
             dma((NB - 1,)),
         ],
         compiler_params=pltpu.CompilerParams(
-            collective_id=0, has_side_effects=True, vmem_limit_bytes=61 * 1024 * 1024
+            collective_id=0, has_side_effects=True, vmem_limit_bytes=48 * 1024 * 1024
         ),
     )(
-        lengths,
-        prefill_flag,
-        cache_slot,
-        slot_owner,
-        hidden_in,
+        table,
         qkv,
         cache,
         out_weight,
     )
+    return (hidden_in.astype(F32) + projected.astype(F32)).astype(BF16)
 
 
 def solution(mesh):

time: 32.6 us -> 29.9 us (0.917)
  local copies, waits for them, and re-layouts: 3.16 us -> 0.01 us
  other arithmetic: 0 us -> 2.9 us
  Pallas kernels: 28.6 us -> 26.2 us
    unnamed x1 -> x2, local copies, waits for them, and re-layouts: 3.16 us -> 0.01 us
    pallas_call x1, Pallas kernels: 28.6 us -> 26.2 us  [local(): pl.pallas_call(functools.partial(kernel, na), out_shape=jax.ShapeDtypeStr...]
    convert_element_type x0 -> x1, other arithmetic: none -> 2.14 us  [local(): return (hidden_in.astype(F32) + projected.astype(F32)).astype(BF16)]
    concatenate x0 -> x1, other arithmetic: none -> 0.77 us  [local(): table = jnp.concatenate([lengths, cache_slot, slot_owner, prefill_flag])]
where the time goes in v3:
time: 29.9 us; the launch traced here: 29.7 us
  Pallas kernels  26.2 us (88%)
  other arithmetic  2.9 us (10%)
  between operations  0.67 us (2%)
    pallas_call x1, Pallas kernels, local(): pl.pallas_call(functools.partial(kernel, na), out_shape=jax.ShapeDtypeStr...  26.2 us
    convert_element_type x1, other arithmetic, local(): return (hidden_in.astype(F32) + projected.astype(F32)).astype(BF16)  2.14 us
    concatenate x1, other arithmetic, local(): table = jnp.concatenate([lengths, cache_slot, slot_owner, prefill_flag])  0.77 us

profile of v3, /device:TPU:0, one launch (start us, length us, event | category | flops | bytes accessed | tf_op | source)
XLA Modules:
  0.0 29.7 jit_solution(1080652764210503250)
XLA Ops:
  0.7 0.8 %pad_add_fusion.table_hbm = s32[13]{0:T(128)S(1)} fusion(s32[1]{0:T(128)S(6)} %copy.9, s32[4]{0:T(128)} %param.14, s32[4]{0:T(128)} %param.13, s32[4]{0:T(128)} %param.11), kind=kLoop, calls=%fused_computation.1 | loop fusion | flops 39 | bytes 104 | tf_op jit(solution)/shard_map/concatenate | solution.py:359
  1.4 0.0 copy-start
  1.4 26.2 %shard_map.82 = bf16[512,2048]{1,0:T(8,128)(2,1)S(1)} custom-call(s32[13]{0:T(128)S(1)} %pad_add_fusion.table_hbm, bf16[512,6144]{1,0:T(8,128)(2,1)} %qkv_hbm.1, bf16[4,128,4096]{2,1,0:T(8,128)(2,1)} %cache_hbm.1, bf16[2048,2048]{1,0:T(8,128)(2,1)} %weight_hbm.1), custom_call_target="tpu_custom_call" | custom-call | tf_op jit(solution)/shard_map/pallas_call | solution.py:360
  27.6 0.0 copy-done
  27.6 2.1 %add_convert_fusion = bf16[512,2048]{1,0:T(8,128)(2,1)} fusion(bf16[512,2048]{1,0:T(8,128)(2,1)S(1)} %shard_map.82, bf16[512,2048]{1,0:T(8,128)(2,1)S(1)} %copy-done), kind=kLoop, calls=%fused_computation | loop fusion | flops 4194304 | bytes 6291456 | tf_op jit(solution)/shard_map/convert_element_type | solution.py:396
Async XLA Ops:
  1.4 26.2 %copy-start = (bf16[512,2048]{1,0:T(8,128)(2,1)S(1)}, bf16[512,2048]{1,0:T(8,128)(2,1)}, u32[]{:S(2)}) copy-start(bf16[512,2048]{1,0:T(8,128)(2,1)} %param.8) | copy-start | bytes 6291460
